TPU v7x, 256 devices: a whole 4x4x8 slice. The times are simulated.
256 devices in a mesh: dp: 8 (over x_lo, y), owner: 8 (over z), context: 4 (over x_hi, core).
Axes of the slice: x: 4 (x_hi: 2, x_lo: 2; x = x_hi * 2 + x_lo), y: 4, z: 8, core: 2. Of those that a mesh axis runs over, the one named last changes fastest.
Arguments:
- grad_partials: bfloat16 [32, 1536, 64, 192], P(('dp', 'context'), None, 'owner')
- assignment: int32 [64, 1], replicated, may hold values from 0 to 7; in each aligned block of 8 rows (0 to 7, 8 to 15, ...) at most 2 rows name the same one
- momentum: float32 [128, 1536, 192], P('owner', ('dp', 'context')), may hold values from -6 to 6
- q_weight: float32 [128, 1536, 192], P('owner', ('dp', 'context')), may hold values from -1.2 to 1.2
- k_weight: float32 [64, 512, 128], P('owner', ('dp', 'context')), may hold values from -6 to 6
- max_logits: float32 [4, 64], P('context'), may hold values from 20 to 400
Outputs:
- momentum_out: float32 [128, 1536, 192], P('owner', ('dp', 'context'))
- q_weight_out: float32 [128, 1536, 192], P('owner', ('dp', 'context'))
- k_weight_out: float32 [64, 512, 128], P('owner', ('dp', 'context'))
Inputs may be any that keep to these rules, and one draw needn't show every extreme that they name: `assignment`: in each aligned block of 8 heads no owner index is named more than 2 times, and some owner index exactly 2 times.
All inputs are finite; a program needn't handle non-finite values.
Results may differ from a plain program's by a relative error of at most 0.0007.
Values may be sent and summed in bfloat16 or wider, within the bound.
A program may use at most 128 MiB of HBM per device.

v0:
```python
import math
import jax
import jax.numpy as jnp
from jax import lax
from jax.sharding import PartitionSpec as P

QR = 1536
QK = 192
ITERS = 2
MOMENTUM_RATE = 0.95
WEIGHT_KEEP = 0.98
LOGIT_CAP = 100.0
QUINTIC_A = 3.4445
QUINTIC_B = -4.775
QUINTIC_C = 2.0315


def routing(assignment, heads_own, per_source):
    target = assignment[:, 0]
    head_index = jnp.arange(target.shape[0], dtype=jnp.int32)
    source_block = head_index // heads_own
    earlier = (
        (source_block[None, :] == source_block[:, None])
        & (head_index[None, :] < head_index[:, None])
        & (target[None, :] == target[:, None])
    )
    position = jnp.sum(earlier.astype(jnp.int32), axis=1)
    return (target, position, source_block * per_source + position)


def refresh(weight, orthogonal, gamma, kn_count):
    step_size = 0.04 * math.sqrt(max(QR, QK))
    column_index = jnp.arange(weight.shape[2])
    column_scale = jnp.where(
        column_index[None, :] < kn_count, jnp.sqrt(gamma)[:, None], gamma[:, None]
    )
    return (WEIGHT_KEEP * weight - step_size * orthogonal.astype(jnp.float32)) * column_scale[
        :, None, :
    ]


def quintic(whole):
    for step in range(ITERS):
        gram_matrix = jnp.einsum("nrk,nrl->nkl", whole, whole, preferred_element_type=jnp.float32)
        polynomial = (
            QUINTIC_B * gram_matrix
            + QUINTIC_C
            * jnp.einsum("nkl,nlm->nkm", gram_matrix, gram_matrix, precision=lax.Precision.HIGHEST)
        ).astype(jnp.bfloat16)
        whole = (
            QUINTIC_A * whole.astype(jnp.float32)
            + jnp.einsum("nrk,nkl->nrl", whole, polynomial, preferred_element_type=jnp.float32)
        ).astype(jnp.bfloat16)
    return whole


def orthogonalize(matrix):
    square_sum = lax.psum(jnp.sum(matrix * matrix, axis=(1, 2)), ("dp", "context"))
    iterate = (matrix / (jnp.sqrt(square_sum) + 1e-07)[:, None, None]).astype(jnp.bfloat16)
    row_count = matrix.shape[1]
    gathered = lax.all_gather(iterate, ("dp", "context"), axis=1, tiled=True)
    gathered = quintic(gathered)
    return lax.dynamic_slice_in_dim(
        gathered, lax.axis_index(("dp", "context")) * row_count, row_count, 1
    )


def body(grad_partials, assignment, momentum, q_weight, k_weight, max_logits):
    heads_own = grad_partials.shape[2]
    slots_own = momentum.shape[0]
    kn_count = k_weight.shape[2]
    per_source = slots_own // lax.axis_size("owner")
    my_owner = lax.axis_index("owner")
    target, position, local_slot = routing(assignment, heads_own, per_source)
    peak_logit = lax.pmax(max_logits[0], "context")
    gamma = jnp.minimum(1.0, LOGIT_CAP / peak_logit)
    partial_value = grad_partials[0]
    grad_rows = lax.psum_scatter(
        partial_value.astype(jnp.float32), ("dp", "context"), scatter_dimension=0, tiled=True
    )
    home_target = lax.dynamic_slice_in_dim(target, my_owner * heads_own, heads_own)
    home_position = lax.dynamic_slice_in_dim(position, my_owner * heads_own, heads_own)
    send_index = home_target * per_source + home_position
    slot_index = jnp.arange(slots_own, dtype=jnp.int32)
    sender = (slot_index[:, None] == send_index[None, :]).astype(jnp.float32)
    owned_mask = (
        (target[None, :] == my_owner) & (local_slot[None, :] == slot_index[:, None])
    ).astype(jnp.float32)
    occupied = (jnp.sum(owned_mask, axis=1) > 0.5)[:, None, None]
    home_gamma = lax.dynamic_slice_in_dim(gamma, my_owner * heads_own, heads_own)
    outgoing = jnp.einsum("qi,rik->qrk", sender, grad_rows, precision=lax.Precision.HIGHEST)
    arrived = lax.all_to_all(outgoing, "owner", split_axis=0, concat_axis=0, tiled=True)
    refreshed = jnp.where(occupied, MOMENTUM_RATE * momentum + arrived, momentum)
    orthogonal = orthogonalize(refreshed)
    slot_gamma = jnp.sum(owned_mask * gamma[None, :], axis=1)
    slot_gamma = jnp.where(occupied[:, 0, 0], slot_gamma, 1.0)
    q_weight_out = jnp.where(
        occupied, refresh(q_weight, orthogonal, slot_gamma, kn_count), q_weight
    )
    k_weight_out = k_weight * jnp.sqrt(home_gamma)[:, None, None]
    return (refreshed, q_weight_out, k_weight_out)


def solution(mesh):
    placed = (
        P(("dp", "context"), None, "owner", None),
        P(),
        P("owner", ("dp", "context"), None),
        P("owner", ("dp", "context"), None),
        P("owner", ("dp", "context"), None),
        P("context", None),
    )
    return jax.shard_map(
        body,
        mesh=mesh,
        in_specs=placed,
        out_specs=(
            P("owner", ("dp", "context"), None),
            P("owner", ("dp", "context"), None),
            P("owner", ("dp", "context"), None),
        ),
        check_vma=False,
    )
```

profile of v0, /device:TPU:1, one launch (start us, length us, event | category | flops | bytes accessed | tf_op | source)
XLA Modules:
  0.0 456.4 jit_solution(1013946448971146130)
XLA Ops:
  7.2 0.0 reduce-scatter.2.cloned.1.call-start
  7.2 9.2 %copy.57 = bf16[1,1536,8,192]{3,2,1,0:T(8,128)(2,1)} copy(bf16[1,1536,8,192]{1,3,2,0:T(8,128)(2,1)} %param.6) | data formatting | bytes 9437184 | tf_op args[0]
  16.4 7.5 %bitcast_convert_fusion = f32[1536,8,192]{2,1,0:T(8,128)} fusion(bf16[1,1536,8,192]{3,2,1,0:T(8,128)(2,1)} %copy.57), kind=kLoop, calls=%fused_computation.4 | loop fusion | flops 2359296 | bytes 14155776 | tf_op jit(solution)/shard_map/convert_element_type | solution.py:79
  23.8 0.0 copy-start.4
  23.8 0.0 reduce-scatter.2.cloned.1.call-update
  23.9 0.0 copy-start.5
  23.9 0.0 copy-start.1
  23.9 0.6 copy-done.4
  24.5 0.2 convert_reduce_fusion
  24.7 0.1 fusion.13
  24.7 175.2 %reduce-scatter.2.cloned.1.call-done = f32[48,8,192]{2,1,0:T(8,128)} async-done(((f32[1536,8,192]{2,1,0:T(8,128)}), f32[48,8,192]{2,1,0:T(8,128)}) %reduce-scatter.2.cloned.1.call-update) | async-done | bytes 294928 | tf_op jit(solution)/shard_map/reduce_scatter | solution.py:78
  199.9 1.6 fusion.8
  201.5 1.3 copy.58
  202.9 0.0 copy-start.3
  202.9 8.6 %all-to-all-start = ((f32[16,48,192]{2,1,0:T(8,128)}), f32[16,48,192]{2,1,0:T(8,128)S(1)}, u32[]{:S(2)}, u32[]{:S(2)}) async-start(f32[16,48,192]{2,1,0:T(8,128)} %copy.58), calls=%async_computation.1 | async-start | bytes 1572864 | tf_op jit(solution)/shard_map/all_to_all | solution.py:92
  211.5 0.0 all-gather.2.cloned.1.call-start
  211.5 0.0 copy-done.5
  211.5 10.9 %pmax.7 = f32[64]{0:T(128)S(1)} all-reduce(f32[64]{0:T(128)S(1)} %bitcast.24), channel_id=1, replica_groups=mesh['dp'=8,'owner'=8,'context'=4] {'context'}, use_global_device_ids=true, to_apply=%region_5.6 | all-reduce | flops 64 | bytes 512 | tf_op jit(solution)/shard_map/pmax | solution.py:75
  222.4 0.1 select_reduce_fusion
  222.5 8.9 %all-to-all-done = f32[16,48,192]{2,1,0:T(8,128)S(1)} async-done(((f32[16,48,192]{2,1,0:T(8,128)}), f32[16,48,192]{2,1,0:T(8,128)S(1)}, u32[]{:S(2)}, u32[]{:S(2)}) %all-to-all-start) | async-done | bytes 589856 | tf_op jit(solution)/shard_map/all_to_all | solution.py:92
  231.4 0.0 copy-done.1
  231.4 0.3 multiply_reduce_fusion
  231.7 0.0 copy-start
  231.8 66.2 %psum.7 = f32[16]{0:T(128)S(1)} all-reduce(f32[16]{0:T(128)S(1)} %get-tuple-element.16), channel_id=1, replica_groups=mesh['dp'=8,'owner'=8,'context'=4] {'dp','context'}, use_global_device_ids=true, to_apply=%region_4.5 | all-reduce | flops 16 | bytes 128 | tf_op jit(solution)/shard_map/psum | solution.py:58
  297.9 0.1 divide_convert_fusion
  298.1 0.9 copy.59
  298.9 0.0 all-gather.2.cloned.1.call-update
  299.0 0.1 dynamic-slice_sqrt_fusion
  299.1 0.1 broadcast_select_fusion
  299.1 0.0 copy-done.3
  299.1 0.7 broadcast_multiply_fusion
  299.9 73.1 %all-gather.2.cloned.1.call-done = bf16[16,1536,192]{2,0,1:T(8,128)(2,1)} async-done(((bf16[16,48,192]{2,0,1:T(8,128)(2,1)}), bf16[16,1536,192]{2,0,1:T(8,128)(2,1)}) %all-gather.2.cloned.1.call-update) | async-done | bytes 9437200 | tf_op jit(solution)/shard_map/all_gather | solution.py:61
  373.0 21.7 %fusion = f32[16,192,192]{2,1,0:T(8,128)S(1)} fusion(bf16[16,1536,192]{2,0,1:T(8,128)(2,1)} %all-gather.2.cloned.1.call-done), kind=kOutput, calls=%fused_computation.1 | convolution fusion | flops 1811939328 | bytes 11796480 | tf_op jit(solution)/shard_map/nrk,nrl->nkl/dot_general | solution.py:44
  394.7 0.0 copy-done
  394.7 3.6 add_convert_fusion.2
  398.3 17.7 %add_convert_fusion = bf16[16,1536,192]{2,1,0:T(8,128)(2,1)} fusion(bf16[16,192,192]{2,1,0:T(8,128)(2,1)S(1)} %add_convert_fusion.2, bf16[16,1536,192]{2,0,1:T(8,128)(2,1)} %all-gather.2.cloned.1.call-done), kind=kOutput, calls=%fused_computation | convolution fusion | flops 1830813696 | bytes 20054016 | tf_op jit(solution)/shard_map/nrk,nkl->nrl/dot_general | solution.py:52
  416.0 11.3 %fusion.15 = f32[16,192,192]{2,1,0:T(8,128)S(1)} fusion(bf16[16,1536,192]{2,1,0:T(8,128)(2,1)} %add_convert_fusion), kind=kOutput, calls=%fused_computation.44 | convolution fusion | flops 1811939328 | bytes 11796480 | tf_op jit(solution)/shard_map/nrk,nrl->nkl/dot_general | solution.py:44
  427.4 3.5 add_convert_fusion.1
  430.8 0.0 copy-start.2
  430.9 16.4 %fusion.16 = f32[16,1536,192]{2,1,0:T(8,128)} fusion(bf16[16,1536,192]{2,1,0:T(8,128)(2,1)} %add_convert_fusion, bf16[16,192,192]{2,1,0:T(8,128)(2,1)S(1)} %add_convert_fusion.1), kind=kOutput, calls=%fused_computation.45 | convolution fusion | flops 1811939328 | bytes 29491200 | tf_op jit(solution)/shard_map/nrk,nkl->nrl/dot_general | solution.py:52
  447.2 0.0 copy-done.2
  447.2 2.4 multiply_select_fusion
  (8 shorter events, 0.0 us)
Async XLA Ops:
  7.2 192.8 %reduce-scatter.2.cloned.1.call-start = ((), (), s32[]{:S(2)}) async-start(), calls=%async_computation.2 | async-start | bytes 12976128 | tf_op jit(solution)/shard_map/reduce_scatter | solution.py:78
  23.8 0.7 copy-start.4
  23.9 187.7 %copy-start.5 = (f32[1,64]{1,0:T(1,128)S(1)}, f32[1,64]{1,0:T(1,128)}, u32[]{:S(2)}) copy-start(f32[1,64]{1,0:T(1,128)} %param.11) | copy-start | bytes 772
  23.9 207.6 %copy-start.1 = (f32[16,48,192]{2,1,0:T(8,128)S(1)}, f32[16,48,192]{2,1,0:T(8,128)}, u32[]{:S(2)}) copy-start(f32[16,48,192]{2,1,0:T(8,128)} %param.8) | copy-start | bytes 1769476
  202.9 96.3 %copy-start.3 = (f32[8,16,128]{2,1,0:T(8,128)S(1)}, f32[8,16,128]{2,1,0:T(8,128)}, u32[]{:S(2)}) copy-start(f32[8,16,128]{2,1,0:T(8,128)} %param.10) | copy-start | bytes 196612
  202.9 28.6 %all-to-all-start = ((f32[16,48,192]{2,1,0:T(8,128)}), f32[16,48,192]{2,1,0:T(8,128)S(1)}, u32[]{:S(2)}, u32[]{:S(2)}) async-start(f32[16,48,192]{2,1,0:T(8,128)} %copy.58), calls=%async_computation.1 | async-start | bytes 1572864 | tf_op jit(solution)/shard_map/all_to_all | solution.py:92
  211.5 161.5 %all-gather.2.cloned.1.call-start = ((), (), s32[]{:S(2)}) async-start(), calls=%async_computation.3 | async-start | bytes 12976128 | tf_op jit(solution)/shard_map/all_gather | solution.py:61
  231.7 163.0 %copy-start = (f32[16,48,192]{2,1,0:T(8,128)}, f32[16,48,192]{2,1,0:T(8,128)S(1)}, u32[]{:S(2)}) copy-start(f32[16,48,192]{2,1,0:T(8,128)S(1)} %get-tuple-element.17) | copy-start | bytes 1769476
  430.8 16.4 %copy-start.2 = (f32[16,48,192]{2,1,0:T(8,128)S(1)}, f32[16,48,192]{2,1,0:T(8,128)}, u32[]{:S(2)}) copy-start(f32[16,48,192]{2,1,0:T(8,128)} %param.9) | copy-start | bytes 1769476
Sparse Core Ops, SparseCore 0:
  24.0 175.8 reduce-scatter.1
  299.1 73.8 all-gather.1
where the time goes:
time: 457 us; the launch traced here: 456 us
  waiting for transfers between devices  257 us (56%)
  blocking collectives  77 us (17%)
  matrix products  75.8 us (17%)
  between operations  14.2 us (3%)
  local copies, waits for them, and re-layouts  12.1 us (3%)
  other arithmetic  11.5 us (3%)
  starting transfers between devices  8.69 us (2%)
    reduce_scatter x1, waiting for transfers between devices, body(): lax.psum_scatter(partial_value.astype(jnp.float32), ('dp', 'context'), sc...  175 us
    all_gather x1, waiting for transfers between devices, orthogonalize(): gathered = lax.all_gather(iterate, ('dp', 'context'), axis=1, tiled=True)  73.1 us
    psum x1, blocking collectives, orthogonalize(): lax.psum(jnp.sum(matrix * matrix, axis=(1, 2)), ('dp', 'context'))  66.2 us
    dot_general x2, matrix products, quintic(): jnp.einsum('nrk,nkl->nrl', whole, polynomial, preferred_element_type=jnp....  34.1 us
    dot_general x2, matrix products, quintic(): jnp.einsum('nrk,nrl->nkl', whole, whole, preferred_element_type=jnp.float32)  33.1 us
    pmax x1, blocking collectives, body(): peak_logit = lax.pmax(max_logits[0], 'context')  10.9 us
    unnamed x13, local copies, waits for them, and re-layouts  9.79 us
  transfers between devices with their start and end apart: 3, of which 3 were waited for; matrix products, arithmetic and copies ran while one was open for 0% of the time, Pallas kernels for 0%

commit v1 on v0

--- a/solution.py
+++ b/solution.py
@@ -55,7 +55,9 @@
 
 
 def orthogonalize(matrix):
-    square_sum = lax.psum(jnp.sum(matrix * matrix, axis=(1, 2)), ("dp", "context"))
+    square_sum = jnp.sum(
+        lax.all_gather(jnp.sum(matrix * matrix, axis=(1, 2)), ("dp", "context")), axis=0
+    )
     iterate = (matrix / (jnp.sqrt(square_sum) + 1e-07)[:, None, None]).astype(jnp.bfloat16)
     row_count = matrix.shape[1]
     gathered = lax.all_gather(iterate, ("dp", "context"), axis=1, tiled=True)

time: 457 us -> 458 us (level)
    unnamed x0 -> x1, blocking collectives: none -> 66.3 us
    psum x1 -> x0, blocking collectives: 66.2 us -> none  [orthogonalize(): lax.psum(jnp.sum(matrix * matrix, axis=(1, 2)), ('dp', 'context'))]
    unnamed x13 -> x18, local copies, waits for them, and re-layouts: 9.79 us -> 10.6 us
where the time goes in v1:
time: 458 us; the launch traced here: 457 us
  waiting for transfers between devices  256 us (56%)
  blocking collectives  77.2 us (17%)
  matrix products  75.9 us (17%)
  between operations  14.8 us (3%)
  local copies, waits for them, and re-layouts  13 us (3%)
  other arithmetic  11.5 us (3%)
  starting transfers between devices  8.69 us (2%)
    reduce_scatter x1, waiting for transfers between devices, body(): lax.psum_scatter(partial_value.astype(jnp.float32), ('dp', 'context'), sc...  175 us
    all_gather x1, waiting for transfers between devices, orthogonalize(): gathered = lax.all_gather(iterate, ('dp', 'context'), axis=1, tiled=True)  73.1 us
    unnamed x1, blocking collectives  66.3 us
    dot_general x2, matrix products, quintic(): jnp.einsum('nrk,nkl->nrl', whole, polynomial, preferred_element_type=jnp....  34.1 us
    dot_general x2, matrix products, quintic(): jnp.einsum('nrk,nrl->nkl', whole, whole, preferred_element_type=jnp.float32)  33.2 us
    pmax x1, blocking collectives, body(): peak_logit = lax.pmax(max_logits[0], 'context')  10.9 us
    unnamed x18, local copies, waits for them, and re-layouts  10.6 us
  transfers between devices with their start and end apart: 3, of which 3 were waited for; matrix products, arithmetic and copies ran while one was open for 0% of the time, Pallas kernels for 0%

profile of v1, /device:TPU:1, one launch (start us, length us, event | category | flops | bytes accessed | tf_op | source)
XLA Modules:
  0.0 457.0 jit_solution(2884689237215560987)
XLA Ops:
  7.2 0.0 reduce-scatter.2.cloned.1.call-start
  7.2 9.2 %copy.73 = bf16[1,1536,8,192]{3,2,1,0:T(8,128)(2,1)} copy(bf16[1,1536,8,192]{1,3,2,0:T(8,128)(2,1)} %param.6) | data formatting | bytes 9437184 | tf_op args[0]
  16.4 7.5 %bitcast_convert_fusion = f32[1536,8,192]{2,1,0:T(8,128)} fusion(bf16[1,1536,8,192]{3,2,1,0:T(8,128)(2,1)} %copy.73), kind=kLoop, calls=%fused_computation.4 | loop fusion | flops 2359296 | bytes 14155776 | tf_op jit(solution)/shard_map/convert_element_type | solution.py:81
  23.8 0.0 copy-start.4
  23.8 0.0 reduce-scatter.2.cloned.1.call-update
  23.9 0.0 copy-start.6
  23.9 0.0 copy-start.5
  23.9 0.0 copy-start.1
  23.9 0.6 copy-done.4
  24.5 0.2 convert_reduce_fusion
  24.7 0.1 fusion.13
  24.7 175.2 %reduce-scatter.2.cloned.1.call-done = f32[48,8,192]{2,1,0:T(8,128)} async-done(((f32[1536,8,192]{2,1,0:T(8,128)}), f32[48,8,192]{2,1,0:T(8,128)}) %reduce-scatter.2.cloned.1.call-update) | async-done | bytes 294928 | tf_op jit(solution)/shard_map/reduce_scatter | solution.py:80
  199.9 1.6 fusion.8
  201.5 1.3 copy.74
  202.9 0.0 copy-start.3
  202.9 8.6 %all-to-all-start = ((f32[16,48,192]{2,1,0:T(8,128)}), f32[16,48,192]{2,1,0:T(8,128)S(1)}, u32[]{:S(2)}, u32[]{:S(2)}) async-start(f32[16,48,192]{2,1,0:T(8,128)} %copy.74), calls=%async_computation.1 | async-start | bytes 1572864 | tf_op jit(solution)/shard_map/all_to_all | solution.py:94
  211.5 0.0 all-gather.3.cloned.1.call-start
  211.5 0.0 copy-done.6
  211.5 0.6 dynamic-slice.1
  212.8 0.0 copy-done.5
  212.8 10.9 %pmax.7 = f32[64]{0:T(128)S(1)} all-reduce(f32[64]{0:T(128)S(1)} %bitcast.25), channel_id=1, replica_groups=mesh['dp'=8,'owner'=8,'context'=4] {'context'}, use_global_device_ids=true, to_apply=%region_5.6 | all-reduce | flops 64 | bytes 512 | tf_op jit(solution)/shard_map/pmax | solution.py:77
  223.7 0.1 select_reduce_fusion
  223.8 7.6 %all-to-all-done = f32[16,48,192]{2,1,0:T(8,128)S(1)} async-done(((f32[16,48,192]{2,1,0:T(8,128)}), f32[16,48,192]{2,1,0:T(8,128)S(1)}, u32[]{:S(2)}, u32[]{:S(2)}) %all-to-all-start) | async-done | bytes 589856 | tf_op jit(solution)/shard_map/all_to_all | solution.py:94
  231.4 0.0 copy-done.1
  231.4 0.3 multiply_reduce_fusion
  231.7 0.0 copy-start
  231.8 0.2 dynamic-update-slice
  232.0 66.3 %all-reduce = f32[512]{0:T(512)S(1)} all-reduce(f32[512]{0:T(512)S(1)} %dynamic-update-slice), channel_id=2, replica_groups=mesh['dp'=8,'owner'=8,'context'=4] {'dp','context'}, use_global_device_ids=true, to_apply=%add | all-reduce | flops 512 | bytes 4096
  298.3 0.1 reshape.112
  298.4 0.1 divide_convert_fusion
  298.6 0.9 copy.75
  299.5 0.0 all-gather.3.cloned.1.call-update
  299.5 0.1 dynamic-slice_sqrt_fusion
  299.6 0.1 broadcast_select_fusion
  299.7 0.0 copy-done.3
  299.7 0.7 broadcast_multiply_fusion
  300.4 73.1 %all-gather.3.cloned.1.call-done = bf16[16,1536,192]{2,0,1:T(8,128)(2,1)} async-done(((bf16[16,48,192]{2,0,1:T(8,128)(2,1)}), bf16[16,1536,192]{2,0,1:T(8,128)(2,1)}) %all-gather.3.cloned.1.call-update) | async-done | bytes 9437200 | tf_op jit(solution)/shard_map/all_gather | solution.py:63
  373.5 21.8 %fusion = f32[16,192,192]{2,1,0:T(8,128)S(1)} fusion(bf16[16,1536,192]{2,0,1:T(8,128)(2,1)} %all-gather.3.cloned.1.call-done), kind=kOutput, calls=%fused_computation.1 | convolution fusion | flops 1811939328 | bytes 11796480 | tf_op jit(solution)/shard_map/nrk,nrl->nkl/dot_general | solution.py:44
  395.3 0.0 copy-done
  395.3 3.6 add_convert_fusion.2
  398.9 17.7 %add_convert_fusion = bf16[16,1536,192]{2,1,0:T(8,128)(2,1)} fusion(bf16[16,192,192]{2,1,0:T(8,128)(2,1)S(1)} %add_convert_fusion.2, bf16[16,1536,192]{2,0,1:T(8,128)(2,1)} %all-gather.3.cloned.1.call-done), kind=kOutput, calls=%fused_computation | convolution fusion | flops 1830813696 | bytes 20054016 | tf_op jit(solution)/shard_map/nrk,nkl->nrl/dot_general | solution.py:52
  416.6 11.4 %fusion.15 = f32[16,192,192]{2,1,0:T(8,128)S(1)} fusion(bf16[16,1536,192]{2,1,0:T(8,128)(2,1)} %add_convert_fusion), kind=kOutput, calls=%fused_computation.44 | convolution fusion | flops 1811939328 | bytes 11796480 | tf_op jit(solution)/shard_map/nrk,nrl->nkl/dot_general | solution.py:44
  428.0 3.5 add_convert_fusion.1
  431.4 0.0 copy-start.2
  431.5 16.4 %fusion.16 = f32[16,1536,192]{2,1,0:T(8,128)} fusion(bf16[16,1536,192]{2,1,0:T(8,128)(2,1)} %add_convert_fusion, bf16[16,192,192]{2,1,0:T(8,128)(2,1)S(1)} %add_convert_fusion.1), kind=kOutput, calls=%fused_computation.45 | convolution fusion | flops 1811939328 | bytes 29491200 | tf_op jit(solution)/shard_map/nrk,nkl->nrl/dot_general | solution.py:52
  447.8 0.0 copy-done.2
  447.8 2.4 multiply_select_fusion
  (10 shorter events, 0.1 us)
Async XLA Ops:
  7.2 192.8 %reduce-scatter.2.cloned.1.call-start = ((), (), s32[]{:S(2)}) async-start(), calls=%async_computation.2 | async-start | bytes 12976128 | tf_op jit(solution)/shard_map/reduce_scatter | solution.py:80
  23.8 0.7 copy-start.4
  23.9 187.7 %copy-start.6 = (u32[256]{0:T(256)S(1)}, u32[256]{0:T(256)}, u32[]{:S(2)}) copy-start(u32[256]{0:T(256)} %constant.82) | copy-start | bytes 3076
  23.9 188.9 %copy-start.5 = (f32[1,64]{1,0:T(1,128)S(1)}, f32[1,64]{1,0:T(1,128)}, u32[]{:S(2)}) copy-start(f32[1,64]{1,0:T(1,128)} %param.11) | copy-start | bytes 772
  23.9 207.5 %copy-start.1 = (f32[16,48,192]{2,1,0:T(8,128)S(1)}, f32[16,48,192]{2,1,0:T(8,128)}, u32[]{:S(2)}) copy-start(f32[16,48,192]{2,1,0:T(8,128)} %param.8) | copy-start | bytes 1769476
  202.9 96.8 %copy-start.3 = (f32[8,16,128]{2,1,0:T(8,128)S(1)}, f32[8,16,128]{2,1,0:T(8,128)}, u32[]{:S(2)}) copy-start(f32[8,16,128]{2,1,0:T(8,128)} %param.10) | copy-start | bytes 196612
  202.9 28.6 %all-to-all-start = ((f32[16,48,192]{2,1,0:T(8,128)}), f32[16,48,192]{2,1,0:T(8,128)S(1)}, u32[]{:S(2)}, u32[]{:S(2)}) async-start(f32[16,48,192]{2,1,0:T(8,128)} %copy.74), calls=%async_computation.1 | async-start | bytes 1572864 | tf_op jit(solution)/shard_map/all_to_all | solution.py:94
  211.5 162.0 %all-gather.3.cloned.1.call-start = ((), (), s32[]{:S(2)}) async-start(), calls=%async_computation.3 | async-start | bytes 12976128 | tf_op jit(solution)/shard_map/all_gather | solution.py:63
  231.7 163.5 %copy-start = (f32[16,48,192]{2,1,0:T(8,128)}, f32[16,48,192]{2,1,0:T(8,128)S(1)}, u32[]{:S(2)}) copy-start(f32[16,48,192]{2,1,0:T(8,128)S(1)} %get-tuple-element.20) | copy-start | bytes 1769476
  431.4 16.4 %copy-start.2 = (f32[16,48,192]{2,1,0:T(8,128)S(1)}, f32[16,48,192]{2,1,0:T(8,128)}, u32[]{:S(2)}) copy-start(f32[16,48,192]{2,1,0:T(8,128)} %param.9) | copy-start | bytes 1769476
Sparse Core Ops, SparseCore 0:
  24.0 175.8 reduce-scatter.1
  299.6 73.8 all-gather.2
